TPU v7x, 32 devices: a whole 2x2x4 slice. The times are simulated.
32 devices in a mesh: dp: 4 (over y, x), expert: 8 (over z, core).
Axes of the slice: x: 2, y: 2, z: 4, core: 2. Of those that a mesh axis runs over, the one named last changes fastest.
Arguments:
- tokens: bfloat16 [4096, 1536], P(('dp', 'expert')), may hold values from -6 to 6
- grad_out: bfloat16 [4096, 1536], P(('dp', 'expert')), may hold values from -6 to 6
- expert_ids: int32 [4096, 4], P(('dp', 'expert')), may hold values from 0 to 7, all different within a row; in each aligned block of 128 rows (0 to 127, 128 to 255, ...) at most 96 rows name the same one
- gate_q: int32 [4096, 4], P(('dp', 'expert')), may hold values from 1 to 65535
- w_up: bfloat16 [8, 1536, 768], P('expert', 'dp'), may hold values from -0.15625 to 0.15625
- w_down: bfloat16 [8, 768, 1536], P('expert', None, 'dp'), may hold values from -0.21875 to 0.21875
Outputs:
- dw_up: bfloat16 [8, 1536, 768], P('expert', 'dp')
- dw_down: bfloat16 [8, 768, 1536], P('expert', None, 'dp')
Inputs may be any that keep to these rules, and one draw needn't show every extreme that they name: `expert_ids`: within the rows of one device no expert is named by more than 96 rows, a bound that some block reaches; the 4 ids of a row differ.
All inputs are finite; a program needn't handle non-finite values.
Results may differ from a plain program's by a relative error of at most 0.0064.
Values may be sent and summed in bfloat16 or wider, within the bound.
No kernel may reach another device: no remote copies, remote signals or barrier semaphores. Data moves between devices by JAX's collectives and lax.ppermute only.
A program may use at most 64 MiB of HBM per device.

v0:
```python
import jax
import jax.numpy as jnp
from jax import lax
from jax.sharding import PartitionSpec as P


def silu_slope(values):
    sigmoid_part = jax.nn.sigmoid(values)
    return sigmoid_part * (1.0 + values * (1.0 - sigmoid_part))


def summed_up(recv_rows, projected_grad):
    first_dims = (((0,), (0,)), ((), ()))
    partial_value = lax.dot_general(
        recv_rows, projected_grad, first_dims, preferred_element_type=jnp.float32
    ).astype(jnp.bfloat16)
    pieces = lax.all_to_all(partial_value[None], "dp", split_axis=1, concat_axis=0, tiled=True)
    return jnp.sum(pieces.astype(jnp.float32), axis=0, keepdims=True).astype(jnp.bfloat16)


def summed_down(activated, grad_rows):
    first_dims = (((0,), (0,)), ((), ()))
    partial_value = lax.dot_general(
        activated, grad_rows, first_dims, preferred_element_type=jnp.float32
    ).astype(jnp.bfloat16)
    pieces = lax.all_to_all(partial_value[None], "dp", split_axis=2, concat_axis=0, tiled=True)
    return jnp.sum(pieces.astype(jnp.float32), axis=0, keepdims=True).astype(jnp.bfloat16)


def shards(tokens, grad_out, expert_ids, gate_q, w_up, w_down):
    devices = lax.axis_size("expert")
    token_count, top_count = expert_ids.shape
    model_width = tokens.shape[1]
    capacity = max(2, token_count * top_count * 3 // (2 * devices))
    slot_expert = expert_ids.reshape(-1)
    onehot_table = (slot_expert[:, None] == jnp.arange(devices, dtype=jnp.int32)[None, :]).astype(
        jnp.int32
    )
    earlier = jnp.cumsum(onehot_table, axis=0) - onehot_table
    slot_rank = jnp.sum(earlier * onehot_table, axis=1)
    slot_target = slot_expert * capacity + slot_rank
    gate_values = gate_q.reshape(-1).astype(jnp.float32) * (1.0 / 65536.0)
    token_rows = jnp.repeat(tokens, top_count, axis=0)
    slot_grads = (
        gate_values[:, None] * jnp.repeat(grad_out, top_count, axis=0).astype(jnp.float32)
    ).astype(jnp.bfloat16)
    empty_rows = jnp.zeros((devices * capacity, model_width), jnp.bfloat16)
    send_tokens = empty_rows.at[slot_target].set(token_rows).reshape(devices, capacity, model_width)
    grad_slots = empty_rows.at[slot_target].set(slot_grads).reshape(devices, capacity, model_width)
    contract_last = (((1,), (1,)), ((), ()))
    up_whole = lax.all_gather(w_up, "dp", axis=1, tiled=True)[0]
    down_whole = lax.all_gather(w_down, "dp", axis=2, tiled=True)[0]
    recv_tokens = lax.all_to_all(send_tokens, "expert", split_axis=0, concat_axis=0, tiled=True)
    recv_rows = recv_tokens.reshape(-1, model_width)
    projected = jnp.dot(recv_rows, up_whole, preferred_element_type=jnp.float32)
    recv_grads = lax.all_to_all(grad_slots, "expert", split_axis=0, concat_axis=0, tiled=True)
    activated = jax.nn.silu(projected).astype(jnp.bfloat16)
    grad_rows = recv_grads.reshape(-1, model_width)
    act_grad = lax.dot_general(
        grad_rows, down_whole, contract_last, preferred_element_type=jnp.float32
    )
    projected_grad = (act_grad * silu_slope(projected)).astype(jnp.bfloat16)
    up_grad = summed_up(recv_rows, projected_grad)
    down_grad = summed_down(activated, grad_rows)
    return (up_grad, down_grad)


def solution(mesh):
    in_specs = (
        P(("dp", "expert"), None),
        P(("dp", "expert"), None),
        P(("dp", "expert"), None),
        P(("dp", "expert"), None),
        P("expert", "dp", None),
        P("expert", None, "dp"),
    )
    out_specs = (P("expert", "dp", None), P("expert", None, "dp"))
    return jax.shard_map(shards, mesh=mesh, in_specs=in_specs, out_specs=out_specs, check_vma=False)
```

profile of v0, /device:TPU:0, one launch (start us, length us, event | category | flops | bytes accessed | tf_op | source)
XLA Modules:
  0.0 307.0 jit_solution(6901323254794781142)
XLA Ops:
  7.2 0.8 copy.25
  8.2 0.7 broadcast_multiply_fusion
  8.9 1.1 reduce-window.6
  10.5 1.4 broadcast_in_dim.22
  12.4 4.7 %scatter_custom_fusion = bf16[768,1536]{1,0:T(8,128)(2,1)} fusion(s32[512]{0:T(512)S(1)} %bitcast.53, bf16[512,1536]{1,0:T(8,128)(2,1)S(1)} %reshape.112, bf16[]{:T(256)} %constant.7.clone.1), kind=kCustom, calls=%fused_computation.18 | custom fusion | bytes 2359298 | tf_op jit(solution)/shard_map/scatter | solution.py:48
  17.1 6.5 %all-to-all-start = ((bf16[8,96,1536]{2,1,0:T(8,128)(2,1)}), bf16[8,96,1536]{2,1,0:T(8,128)(2,1)}, u32[]{:S(2)}, u32[]{:S(2)}) async-start(bf16[8,96,1536]{2,1,0:T(8,128)(2,1)} %bitcast.4), calls=%async_computation | async-start | bytes 4718592 | tf_op jit(solution)/shard_map/all_to_all | solution.py:53
  24.7 2.3 convert_element_type.78
  27.2 6.0 %scatter_custom_fusion.1 = bf16[768,1536]{1,0:T(8,128)(2,1)} fusion(s32[512]{0:T(512)S(1)} %bitcast.54, f32[512,1536]{1,0:T(8,128)} %convert_element_type.78, f32[512]{0:T(512)S(1)} %mul.59, bf16[]{:T(256)} %constant.7.clone.1), kind=kCustom, calls=%fused_computation.14 | custom fusion | flops 1572864 | bytes 5507074 | tf_op jit(solution)/shard_map/scatter | solution.py:49
  33.3 45.1 %all-to-all-done = bf16[8,96,1536]{2,1,0:T(8,128)(2,1)} async-done(((bf16[8,96,1536]{2,1,0:T(8,128)(2,1)}), bf16[8,96,1536]{2,1,0:T(8,128)(2,1)}, u32[]{:S(2)}, u32[]{:S(2)}) %all-to-all-start) | async-done | bytes 2359328 | tf_op jit(solution)/shard_map/all_to_all | solution.py:53
  78.3 3.6 %all-to-all-start.1 = ((bf16[8,96,1536]{2,1,0:T(8,128)(2,1)}), bf16[8,96,1536]{2,1,0:T(8,128)(2,1)S(1)}, u32[]{:S(2)}, u32[]{:S(2)}) async-start(bf16[8,96,1536]{2,1,0:T(8,128)(2,1)} %bitcast.6), calls=%async_computation.1 | async-start | bytes 4718592 | tf_op jit(solution)/shard_map/all_to_all | solution.py:56
  82.7 5.8 %fusion.2 = f32[768,768]{1,0:T(8,128)} fusion(bf16[768,1536]{1,0:T(8,128)(2,1)} %bitcast.5, bf16[1,1536,768]{2,1,0:T(8,128)(2,1)} %all-gather.5.cloned.1.call-done), kind=kOutput, calls=%fused_computation.7 | convolution fusion | flops 1811939328 | bytes 7077888 | tf_op jit(solution)/shard_map/dot_general | solution.py:55
  88.5 34.7 %all-gather.3.cloned.1.call-done = bf16[1,768,1536]{2,1,0:T(8,128)(2,1)} async-done(((bf16[1,768,384]{2,1,0:T(8,128)(2,1)}), bf16[1,768,1536]{2,1,0:T(8,128)(2,1)}) %all-gather.3.cloned.1.call-update) | async-done | bytes 2359312 | tf_op jit(solution)/shard_map/all_gather | solution.py:52
  123.2 13.3 %all-to-all-done.1 = bf16[8,96,1536]{2,1,0:T(8,128)(2,1)S(1)} async-done(((bf16[8,96,1536]{2,1,0:T(8,128)(2,1)}), bf16[8,96,1536]{2,1,0:T(8,128)(2,1)S(1)}, u32[]{:S(2)}, u32[]{:S(2)}) %all-to-all-start.1) | async-done | bytes 2359328 | tf_op jit(solution)/shard_map/all_to_all | solution.py:56
  136.5 1.4 copy-done
  137.9 8.2 %fusion = bf16[1,1536,768]{2,1,0:T(8,128)(2,1)S(1)} fusion(bf16[768,1536]{1,0:T(8,128)(2,1)} %bitcast.5, f32[768,768]{1,0:T(8,128)} %fusion.2, bf16[768,1536]{1,0:T(8,128)(2,1)} %bitcast.48, bf16[1,768,1536]{2,1,0:T(8,128)(2,1)} %all-gather.3.cloned.1.call-done), kind=kOutput, calls=%fused_computation.5 | convolution fusion | flops 3630366720 | bytes 11796480 | tf_op jit(solution)/shard_map/dot_general | solution.py:14
  146.1 33.8 %copy.34 = bf16[1,1536,768]{2,0,1:T(2,128)(2,1)} copy(bf16[1,1536,768]{2,1,0:T(8,128)(2,1)S(1)} %fusion) | data formatting | bytes 4718592 | tf_op jit(solution)/shard_map/broadcast_in_dim | solution.py:17
  180.4 24.1 %reduce.7 = bf16[1536,768]{1,0:T(8,128)(2,1)S(1)} reduce(bf16[1536,1,768]{2,1,0:T(2,128)(2,1)} %bitcast.42, bf16[]{:T(256)} %broadcast.72), dimensions={1}, to_apply=%bitcast.41.reduce_sub_computation | reduce | bytes 4718594
  204.5 2.3 reshape.129
  206.8 3.9 %all-to-all-start.2 = ((bf16[4,2,147456]{2,1,0:T(2,128)(2,1)}), bf16[4,2,147456]{2,1,0:T(2,128)(2,1)S(1)}, u32[]{:S(2)}, u32[]{:S(2)}) async-start(bf16[4,2,147456]{2,1,0:T(2,128)(2,1)} %reshape.129), calls=%async_computation.2 | async-start | bytes 4718592 | tf_op jit(solution)/shard_map/all_to_all | solution.py:17
  210.6 5.9 %fusion.1 = bf16[1,768,1536]{2,1,0:T(8,128)(2,1)} fusion(bf16[768,1536]{1,0:T(8,128)(2,1)} %bitcast.49, f32[768,768]{1,0:T(8,128)} %fusion.2), kind=kOutput, calls=%fused_computation.6 | convolution fusion | flops 1816068096 | bytes 7077888 | tf_op jit(solution)/shard_map/dot_general | solution.py:23
  216.5 12.1 %copy.29 = bf16[1,768,1536]{1,0,2:T(2,128)(2,1)} copy(bf16[1,768,1536]{2,1,0:T(8,128)(2,1)} %fusion.1) | data formatting | bytes 4718592 | tf_op jit(solution)/shard_map/broadcast_in_dim | solution.py:26
  228.6 25.5 %reduce.8 = bf16[1536,768]{1,0:T(8,128)(2,1)} reduce(bf16[1536,1,768]{2,1,0:T(2,128)(2,1)} %bitcast.43, bf16[]{:T(256)} %broadcast.72), dimensions={1}, to_apply=%bitcast.34.reduce_sub_computation | reduce | bytes 4718594
  254.1 4.1 %reshape.131 = bf16[4,2,147456]{2,1,0:T(2,128)(2,1)} reshape(bf16[1536,768]{1,0:T(8,128)(2,1)} %reduce.8) | data formatting | bytes 4718592
  258.2 4.5 %all-to-all-start.3 = ((bf16[4,2,147456]{2,1,0:T(2,128)(2,1)}), bf16[4,2,147456]{2,1,0:T(2,128)(2,1)}, u32[]{:S(2)}, u32[]{:S(2)}) async-start(bf16[4,2,147456]{2,1,0:T(2,128)(2,1)} %reshape.131), calls=%async_computation.3 | async-start | bytes 4718592 | tf_op jit(solution)/shard_map/all_to_all | solution.py:26
  262.7 3.6 %reshape.130 = bf16[1536,1,768]{2,1,0:T(2,128)(2,1)} reshape(bf16[4,2,147456]{2,1,0:T(2,128)(2,1)S(1)} %all-to-all-done.2) | data formatting | bytes 4718592
  266.3 2.7 copy.31
  269.0 1.3 reduce.4
  270.3 20.1 %all-to-all-done.3 = bf16[4,2,147456]{2,1,0:T(2,128)(2,1)} async-done(((bf16[4,2,147456]{2,1,0:T(2,128)(2,1)}), bf16[4,2,147456]{2,1,0:T(2,128)(2,1)}, u32[]{:S(2)}, u32[]{:S(2)}) %all-to-all-start.3) | async-done | bytes 2359328 | tf_op jit(solution)/shard_map/all_to_all | solution.py:26
  290.5 5.2 %reshape.132 = bf16[1536,1,768]{2,1,0:T(2,128)(2,1)} reshape(bf16[4,2,147456]{2,1,0:T(2,128)(2,1)} %all-to-all-done.3) | data formatting | bytes 4718592
  295.6 2.7 copy.32
  298.4 0.7 reduce_sum.35
  299.1 1.1 copy.30
  (27 shorter events, 3.8 us)
Async XLA Ops:
  17.1 7.2 %copy-start.1 = (bf16[128,1536]{1,0:T(8,128)(2,1)S(1)}, bf16[128,1536]{1,0:T(8,128)(2,1)}, u32[]{:S(2)}) copy-start(bf16[128,1536]{1,0:T(8,128)(2,1)} %param.7) | copy-start | bytes 1179652
  17.1 61.2 %all-to-all-start = ((bf16[8,96,1536]{2,1,0:T(8,128)(2,1)}), bf16[8,96,1536]{2,1,0:T(8,128)(2,1)}, u32[]{:S(2)}, u32[]{:S(2)}) async-start(bf16[8,96,1536]{2,1,0:T(8,128)(2,1)} %bitcast.4), calls=%async_computation | async-start | bytes 4718592 | tf_op jit(solution)/shard_map/all_to_all | solution.py:53
  23.6 59.2 %all-gather.5.cloned.1.call-start = ((), (), s32[]{:S(2)}) async-start(), calls=%async_computation.5 | async-start | bytes 2949120 | tf_op jit(solution)/shard_map/all_gather | solution.py:51
  24.7 2.3 copy-start.2
  78.3 58.2 %all-to-all-start.1 = ((bf16[8,96,1536]{2,1,0:T(8,128)(2,1)}), bf16[8,96,1536]{2,1,0:T(8,128)(2,1)S(1)}, u32[]{:S(2)}, u32[]{:S(2)}) async-start(bf16[8,96,1536]{2,1,0:T(8,128)(2,1)} %bitcast.6), calls=%async_computation.1 | async-start | bytes 4718592 | tf_op jit(solution)/shard_map/all_to_all | solution.py:56
  81.9 41.3 %all-gather.3.cloned.1.call-start = ((), (), s32[]{:S(2)}) async-start(), calls=%async_computation.4 | async-start | bytes 2949120 | tf_op jit(solution)/shard_map/all_gather | solution.py:52
  136.5 1.4 copy-start
  206.8 51.5 %all-to-all-start.2 = ((bf16[4,2,147456]{2,1,0:T(2,128)(2,1)}), bf16[4,2,147456]{2,1,0:T(2,128)(2,1)S(1)}, u32[]{:S(2)}, u32[]{:S(2)}) async-start(bf16[4,2,147456]{2,1,0:T(2,128)(2,1)} %reshape.129), calls=%async_computation.2 | async-start | bytes 4718592 | tf_op jit(solution)/shard_map/all_to_all | solution.py:17
  258.2 32.2 %all-to-all-start.3 = ((bf16[4,2,147456]{2,1,0:T(2,128)(2,1)}), bf16[4,2,147456]{2,1,0:T(2,128)(2,1)}, u32[]{:S(2)}, u32[]{:S(2)}) async-start(bf16[4,2,147456]{2,1,0:T(2,128)(2,1)} %reshape.131), calls=%async_computation.3 | async-start | bytes 4718592 | tf_op jit(solution)/shard_map/all_to_all | solution.py:26
Sparse Core Ops, SparseCore 0:
  26.2 38.7 all-gather.4
  84.6 38.5 all-gather.2
where the time goes:
time: 308 us; the launch traced here: 307 us
  waiting for transfers between devices  114 us (37%)
  local copies, waits for them, and re-layouts  80.2 us (26%)
  other arithmetic  59.7 us (19%)
  matrix products  19.9 us (6%)
  starting transfers between devices  18.7 us (6%)
  between operations  14.2 us (5%)
    unnamed x2, other arithmetic  49.6 us
    all_to_all x1, waiting for transfers between devices, shards(): lax.all_to_all(send_tokens, 'expert', split_axis=0, concat_axis=0, tiled=...  45.1 us
    all_gather x1, waiting for transfers between devices, shards(): down_whole = lax.all_gather(w_down, 'dp', axis=2, tiled=True)[0]  34.7 us
    broadcast_in_dim x1, local copies, waits for them, and re-layouts, summed_up(): partial_value[None]  33.8 us
    unnamed x15, local copies, waits for them, and re-layouts  24.3 us
    all_to_all x1, waiting for transfers between devices, summed_down(): lax.all_to_all(partial_value[None], 'dp', split_axis=2, concat_axis=0, ti...  20.1 us
    all_to_all x1, waiting for transfers between devices, shards(): lax.all_to_all(grad_slots, 'expert', split_axis=0, concat_axis=0, tiled=T...  13.3 us
    broadcast_in_dim x1, local copies, waits for them, and re-layouts, summed_down(): partial_value[None]  12.1 us
  transfers between devices with their start and end apart: 6, of which 4 were waited for; matrix products, arithmetic and copies ran while one was open for 23% of the time, Pallas kernels for 0%

commit v1 on v0

--- a/solution.py
+++ b/solution.py
@@ -23,7 +23,15 @@
     partial_value = lax.dot_general(
         activated, grad_rows, first_dims, preferred_element_type=jnp.float32
     ).astype(jnp.bfloat16)
-    pieces = lax.all_to_all(partial_value[None], "dp", split_axis=2, concat_axis=0, tiled=True)
+    pieces = jnp.concatenate(
+        lax.all_to_all(
+            jnp.stack(jnp.split(partial_value[None], lax.psum(1, "dp"), axis=2)),
+            axis_name="dp",
+            split_axis=0,
+            concat_axis=0,
+        ),
+        axis=0,
+    )
     return jnp.sum(pieces.astype(jnp.float32), axis=0, keepdims=True).astype(jnp.bfloat16)
 
 

time: 308 us -> 280 us (0.909)
  local copies, waits for them, and re-layouts: 80.2 us -> 55.3 us
  other arithmetic: 59.7 us -> 38.3 us
  waiting for transfers between devices: 114 us -> 135 us
    unnamed x2 -> x1, other arithmetic: 49.6 us -> 24.1 us
    all_to_all x1, waiting for transfers between devices: 0.01 us -> 21 us  [summed_up(): lax.all_to_all(partial_value[None], 'dp', split_axis=1, concat_axis=0, ti...]
    unnamed x15 -> x11, local copies, waits for them, and re-layouts: 24.3 us -> 11.2 us
    broadcast_in_dim x1 -> x0, local copies, waits for them, and re-layouts: 12.1 us -> none  [summed_down(): partial_value[None]]
  transfers between devices with their start and end apart: 6 -> 6, of which waited for: 4 -> 5; matrix products, arithmetic and copies ran while one was open for 23% -> 10% of each run, Pallas kernels for 0% -> 0%
where the time goes in v1:
time: 280 us
  waiting for transfers between devices  135 us (48%)
  local copies, waits for them, and re-layouts  55.3 us (20%)
  other arithmetic  38.3 us (14%)
  starting transfers between devices  18.6 us (7%)
  matrix products  18.4 us (7%)
  between operations  14.2 us (5%)
    all_to_all x1, waiting for transfers between devices, shards(): lax.all_to_all(send_tokens, 'expert', split_axis=0, concat_axis=0, tiled=...  45.1 us
    all_gather x1, waiting for transfers between devices, shards(): down_whole = lax.all_gather(w_down, 'dp', axis=2, tiled=True)[0]  34.7 us
    broadcast_in_dim x1, local copies, waits for them, and re-layouts, summed_up(): partial_value[None]  33.8 us
    unnamed x1, other arithmetic  24.1 us
    all_to_all x1, waiting for transfers between devices, summed_up(): lax.all_to_all(partial_value[None], 'dp', split_axis=1, concat_axis=0, ti...  21 us
    all_to_all x1, waiting for transfers between devices, summed_down(): lax.all_to_all(jnp.stack(jnp.split(partial_value[None], lax.psum(1, 'dp')...  19.6 us
    all_to_all x1, waiting for transfers between devices, shards(): lax.all_to_all(grad_slots, 'expert', split_axis=0, concat_axis=0, tiled=T...  13.3 us
    unnamed x11, local copies, waits for them, and re-layouts  11.2 us
  transfers between devices with their start and end apart: 6, of which 5 were waited for; matrix products, arithmetic and copies ran while one was open for 10% of the time, Pallas kernels for 0%

profile of v1, /device:TPU:0, one launch (start us, length us, event | category | flops | bytes accessed | tf_op | source)
XLA Modules:
  0.0 279.6 jit_solution(2208196081923102020)
XLA Ops:
  7.2 0.7 broadcast_multiply_fusion
  7.8 0.8 copy.18
  9.1 1.1 reduce-window.6
  10.5 1.4 broadcast_in_dim.22
  12.4 4.7 %scatter_custom_fusion = bf16[768,1536]{1,0:T(8,128)(2,1)} fusion(s32[512]{0:T(512)S(1)} %bitcast.55, bf16[512,1536]{1,0:T(8,128)(2,1)S(1)} %reshape.112, bf16[]{:T(256)} %constant.7.clone.1), kind=kCustom, calls=%fused_computation.19 | custom fusion | bytes 2359298 | tf_op jit(solution)/shard_map/scatter | solution.py:56
  17.1 6.5 %all-to-all-start = ((bf16[8,96,1536]{2,1,0:T(8,128)(2,1)}), bf16[8,96,1536]{2,1,0:T(8,128)(2,1)}, u32[]{:S(2)}, u32[]{:S(2)}) async-start(bf16[8,96,1536]{2,1,0:T(8,128)(2,1)} %bitcast.4), calls=%async_computation | async-start | bytes 4718592 | tf_op jit(solution)/shard_map/all_to_all | solution.py:61
  23.6 0.7 all-gather.5.cloned.1.call-update
  24.3 0.4 broadcast_in_dim.23
  24.8 2.3 convert_element_type.78
  27.2 6.0 %scatter_custom_fusion.1 = bf16[768,1536]{1,0:T(8,128)(2,1)} fusion(s32[512]{0:T(512)S(1)} %bitcast.56, f32[512,1536]{1,0:T(8,128)} %convert_element_type.78, f32[512]{0:T(512)S(1)} %mul.59, bf16[]{:T(256)} %constant.7.clone.1), kind=kCustom, calls=%fused_computation.15 | custom fusion | flops 1572864 | bytes 5507074 | tf_op jit(solution)/shard_map/scatter | solution.py:57
  33.3 45.1 %all-to-all-done = bf16[8,96,1536]{2,1,0:T(8,128)(2,1)} async-done(((bf16[8,96,1536]{2,1,0:T(8,128)(2,1)}), bf16[8,96,1536]{2,1,0:T(8,128)(2,1)}, u32[]{:S(2)}, u32[]{:S(2)}) %all-to-all-start) | async-done | bytes 2359328 | tf_op jit(solution)/shard_map/all_to_all | solution.py:61
  78.3 3.6 %all-to-all-start.1 = ((bf16[8,96,1536]{2,1,0:T(8,128)(2,1)}), bf16[8,96,1536]{2,1,0:T(8,128)(2,1)S(1)}, u32[]{:S(2)}, u32[]{:S(2)}) async-start(bf16[8,96,1536]{2,1,0:T(8,128)(2,1)} %bitcast.6), calls=%async_computation.1 | async-start | bytes 4718592 | tf_op jit(solution)/shard_map/all_to_all | solution.py:64
  82.2 0.5 all-gather.3.cloned.1.call-update
  82.7 5.8 %fusion.2 = f32[768,768]{1,0:T(8,128)} fusion(bf16[768,1536]{1,0:T(8,128)(2,1)} %bitcast.5, bf16[1,1536,768]{2,1,0:T(8,128)(2,1)} %all-gather.5.cloned.1.call-done), kind=kOutput, calls=%fused_computation.8 | convolution fusion | flops 1811939328 | bytes 7077888 | tf_op jit(solution)/shard_map/dot_general | solution.py:63
  88.5 34.7 %all-gather.3.cloned.1.call-done = bf16[1,768,1536]{2,1,0:T(8,128)(2,1)} async-done(((bf16[1,768,384]{2,1,0:T(8,128)(2,1)}), bf16[1,768,1536]{2,1,0:T(8,128)(2,1)}) %all-gather.3.cloned.1.call-update) | async-done | bytes 2359312 | tf_op jit(solution)/shard_map/all_gather | solution.py:60
  123.2 13.3 %all-to-all-done.1 = bf16[8,96,1536]{2,1,0:T(8,128)(2,1)S(1)} async-done(((bf16[8,96,1536]{2,1,0:T(8,128)(2,1)}), bf16[8,96,1536]{2,1,0:T(8,128)(2,1)S(1)}, u32[]{:S(2)}, u32[]{:S(2)}) %all-to-all-start.1) | async-done | bytes 2359328 | tf_op jit(solution)/shard_map/all_to_all | solution.py:64
  136.5 1.5 copy-done
  138.0 8.2 %fusion = bf16[1,1536,768]{2,1,0:T(8,128)(2,1)S(1)} fusion(bf16[768,1536]{1,0:T(8,128)(2,1)} %bitcast.5, f32[768,768]{1,0:T(8,128)} %fusion.2, bf16[768,1536]{1,0:T(8,128)(2,1)} %bitcast.50, bf16[1,768,1536]{2,1,0:T(8,128)(2,1)} %all-gather.3.cloned.1.call-done), kind=kOutput, calls=%fused_computation.5 | convolution fusion | flops 3630366720 | bytes 11796480 | tf_op jit(solution)/shard_map/dot_general | solution.py:14
  146.2 33.8 %copy.24 = bf16[1,1536,768]{2,0,1:T(2,128)(2,1)} copy(bf16[1,1536,768]{2,1,0:T(8,128)(2,1)S(1)} %fusion) | data formatting | bytes 4718592 | tf_op jit(solution)/shard_map/broadcast_in_dim | solution.py:17
  180.0 0.5 broadcast.72
  180.5 24.1 %reduce.5 = bf16[1536,768]{1,0:T(8,128)(2,1)S(1)} reduce(bf16[1536,1,768]{2,1,0:T(2,128)(2,1)} %bitcast.47, bf16[]{:T(256)} %broadcast.72), dimensions={1}, to_apply=%bitcast.46.reduce_sub_computation | reduce | bytes 4718594
  204.6 2.2 reshape.129
  206.8 3.7 %all-to-all-start.2 = ((bf16[4,2,147456]{2,1,0:T(2,128)(2,1)}), bf16[4,2,147456]{2,1,0:T(2,128)(2,1)S(1)}, u32[]{:S(2)}, u32[]{:S(2)}) async-start(bf16[4,2,147456]{2,1,0:T(2,128)(2,1)} %reshape.129), calls=%async_computation.2 | async-start | bytes 4718592 | tf_op jit(solution)/shard_map/all_to_all | solution.py:17
  210.5 4.4 %fusion.1 = bf16[1,768,1536]{2,1,0:T(8,128)(2,1)S(1)} fusion(bf16[768,1536]{1,0:T(8,128)(2,1)} %bitcast.51, f32[768,768]{1,0:T(8,128)} %fusion.2), kind=kOutput, calls=%fused_computation.6 | convolution fusion | flops 1816068096 | bytes 7077888 | tf_op jit(solution)/shard_map/dot_general | solution.py:23
  215.2 1.8 pad_maximum_fusion
  217.0 21.0 %all-to-all-done.2 = bf16[4,2,147456]{2,1,0:T(2,128)(2,1)S(1)} async-done(((bf16[4,2,147456]{2,1,0:T(2,128)(2,1)}), bf16[4,2,147456]{2,1,0:T(2,128)(2,1)S(1)}, u32[]{:S(2)}, u32[]{:S(2)}) %all-to-all-start.2) | async-done | bytes 2359328 | tf_op jit(solution)/shard_map/all_to_all | solution.py:17
  238.1 4.5 %all-to-all-start.3 = ((bf16[4,1,768,384]{3,2,1,0:T(8,128)(2,1)}), bf16[4,1,768,384]{3,2,1,0:T(8,128)(2,1)}, u32[]{:S(2)}, u32[]{:S(2)}) async-start(bf16[4,1,768,384]{3,2,1,0:T(8,128)(2,1)} %pad_maximum_fusion), calls=%async_computation.3 | async-start | bytes 4718592 | tf_op jit(solution)/shard_map/all_to_all | solution.py:27
  242.6 3.6 %reshape.130 = bf16[1536,1,768]{2,1,0:T(2,128)(2,1)} reshape(bf16[4,2,147456]{2,1,0:T(2,128)(2,1)S(1)} %all-to-all-done.2) | data formatting | bytes 4718592
  246.1 2.7 copy.22
  248.9 1.3 reduce.2
  250.2 19.6 %all-to-all-done.3 = bf16[4,1,768,384]{3,2,1,0:T(8,128)(2,1)} async-done(((bf16[4,1,768,384]{3,2,1,0:T(8,128)(2,1)}), bf16[4,1,768,384]{3,2,1,0:T(8,128)(2,1)}, u32[]{:S(2)}, u32[]{:S(2)}) %all-to-all-start.3) | async-done | bytes 2359328 | tf_op jit(solution)/shard_map/all_to_all | solution.py:27
  269.8 3.0 %reduce_sum.35 = bf16[768,384]{1,0:T(8,128)(2,1)} reduce(bf16[4,1,768,384]{3,2,1,0:T(8,128)(2,1)} %all-to-all-done.3, bf16[]{:T(256)} %constant.7.clone.1), dimensions={0,1}, to_apply=%region_6.7 | reduce | flops 884736 | bytes 2949122 | tf_op jit(solution)/shard_map/reduce_sum | solution.py:35
  (23 shorter events, 1.9 us)
Async XLA Ops:
  17.1 7.2 %copy-start.1 = (bf16[128,1536]{1,0:T(8,128)(2,1)S(1)}, bf16[128,1536]{1,0:T(8,128)(2,1)}, u32[]{:S(2)}) copy-start(bf16[128,1536]{1,0:T(8,128)(2,1)} %param.7) | copy-start | bytes 1179652
  17.1 61.2 %all-to-all-start = ((bf16[8,96,1536]{2,1,0:T(8,128)(2,1)}), bf16[8,96,1536]{2,1,0:T(8,128)(2,1)}, u32[]{:S(2)}, u32[]{:S(2)}) async-start(bf16[8,96,1536]{2,1,0:T(8,128)(2,1)} %bitcast.4), calls=%async_computation | async-start | bytes 4718592 | tf_op jit(solution)/shard_map/all_to_all | solution.py:61
  23.6 59.2 %all-gather.5.cloned.1.call-start = ((), (), s32[]{:S(2)}) async-start(), calls=%async_computation.5 | async-start | bytes 2949120 | tf_op jit(solution)/shard_map/all_gather | solution.py:59
  24.7 2.3 copy-start.2
  78.3 58.2 %all-to-all-start.1 = ((bf16[8,96,1536]{2,1,0:T(8,128)(2,1)}), bf16[8,96,1536]{2,1,0:T(8,128)(2,1)S(1)}, u32[]{:S(2)}, u32[]{:S(2)}) async-start(bf16[8,96,1536]{2,1,0:T(8,128)(2,1)} %bitcast.6), calls=%async_computation.1 | async-start | bytes 4718592 | tf_op jit(solution)/shard_map/all_to_all | solution.py:64
  82.0 41.3 %all-gather.3.cloned.1.call-start = ((), (), s32[]{:S(2)}) async-start(), calls=%async_computation.4 | async-start | bytes 2949120 | tf_op jit(solution)/shard_map/all_gather | solution.py:60
  136.5 1.5 copy-start
  206.8 31.3 %all-to-all-start.2 = ((bf16[4,2,147456]{2,1,0:T(2,128)(2,1)}), bf16[4,2,147456]{2,1,0:T(2,128)(2,1)S(1)}, u32[]{:S(2)}, u32[]{:S(2)}) async-start(bf16[4,2,147456]{2,1,0:T(2,128)(2,1)} %reshape.129), calls=%async_computation.2 | async-start | bytes 4718592 | tf_op jit(solution)/shard_map/all_to_all | solution.py:17
  238.1 31.7 %all-to-all-start.3 = ((bf16[4,1,768,384]{3,2,1,0:T(8,128)(2,1)}), bf16[4,1,768,384]{3,2,1,0:T(8,128)(2,1)}, u32[]{:S(2)}, u32[]{:S(2)}) async-start(bf16[4,1,768,384]{3,2,1,0:T(8,128)(2,1)} %pad_maximum_fusion), calls=%async_computation.3 | async-start | bytes 4718592 | tf_op jit(solution)/shard_map/all_to_all | solution.py:27
Sparse Core Ops, SparseCore 0:
  26.2 38.7 all-gather.4
  84.6 38.5 all-gather.2
